TPU v7x, 32 devices: a whole 2x2x4 slice. The times are simulated.
32 devices in a mesh: req: 8 (over z, x), tp: 4 (over y, core).
Axes of the slice: x: 2, y: 2, z: 4, core: 2. Of those that a mesh axis runs over, the one named last changes fastest.
Arguments:
- hidden: bfloat16 [512, 2048], P('req')
- norm_gain: float32 [2048], replicated, may hold values from 0.5 to 1.5
- head_weight: bfloat16 [2048, 12288], P(None, ('req', 'tp'))
- targets: int32 [512], P('req'), may hold values from 0 to 12287
- pad_mask: int32 [512], P('req'), may hold values 0 or 1
Outputs:
- logprob: float32 [512], P('req')
- entropy: float32 [512], P('req')
All inputs are finite; a program needn't handle non-finite values. No bound on the sum of `pad_mask` on one device may be relied on, other than what follows from the above.
Results may differ from a plain program's by a relative error of at most 0.0012.
Values may be sent and summed in bfloat16 or wider, within the bound.
A program may use at most 128 MiB of HBM per device.

v0:
```python
import jax
import jax.numpy as jnp
from jax import lax
from jax.sharding import PartitionSpec as P


def combined_all(value, axis, join):
    pieces = jax.tree.map(lambda part: lax.all_gather(part, axis), value)
    head = jax.tree.map(lambda part: part[0], pieces)
    tail = jax.tree.map(lambda part: part[1:], pieces)
    subtotal, _ = lax.scan(lambda subtotal, slab: (join(subtotal, slab), None), head, tail)
    return subtotal


def combine_stats(earlier, later):
    top_a, total_a, weighted_a, picked_a = earlier
    top_b, total_b, weighted_b, picked_b = later
    top_new = jnp.maximum(top_a, top_b)
    scale_a = jnp.exp(top_a - top_new)
    scale_b = jnp.exp(top_b - top_new)
    return (
        top_new,
        total_a * scale_a + total_b * scale_b,
        weighted_a * scale_a + weighted_b * scale_b,
        picked_a + picked_b,
    )


def body(hidden, norm_gain, head_weight, targets, pad_mask):
    slots = hidden.shape[0]
    voc_local = head_weight.shape[1]
    tp_count = lax.axis_size("tp")
    voc_start = (lax.axis_index("req") * tp_count + lax.axis_index("tp")) * voc_local
    wide = hidden.astype(jnp.float32)
    scale = lax.rsqrt(jnp.mean(wide * wide, axis=1, keepdims=True) + 1e-05)
    normed = (wide * scale * norm_gain[None, :]).astype(jnp.bfloat16)
    columns = lax.broadcasted_iota(jnp.int32, (1, voc_local), 1)
    all_targets = lax.all_gather(targets, "req", axis=0, tiled=True)
    logits = jnp.dot(
        lax.all_gather(normed, "req", axis=0, tiled=True),
        head_weight,
        preferred_element_type=jnp.float32,
    )
    top_row = jnp.max(logits, axis=1)
    expo = jnp.exp(logits - top_row[:, None])
    local = all_targets - voc_start
    picked_row = jnp.sum(jnp.where(columns == local[:, None], logits, jnp.float32(0.0)), axis=1)
    parts = (top_row, jnp.sum(expo, axis=1), jnp.sum(expo * logits, axis=1), picked_row)
    stats = tuple((fresh for fresh in parts))
    merged = combined_all(stats, ("req", "tp"), combine_stats)
    own_start = lax.axis_index("req") * slots
    top_all, total_all, weighted_all, picked_all = tuple(
        (lax.dynamic_slice_in_dim(whole, own_start, slots, 0) for whole in merged)
    )
    lse = top_all + jnp.log(total_all)
    live = pad_mask.astype(jnp.float32)
    logprob = (picked_all - lse) * live
    entropy = (lse - weighted_all / total_all) * live
    return (logprob, entropy)


def solution(mesh):
    return jax.shard_map(
        body,
        mesh=mesh,
        in_specs=(P("req", None), P(), P(None, ("req", "tp")), P("req"), P("req")),
        out_specs=(P("req"), P("req")),
        check_vma=False,
    )
```

profile of v0, /device:TPU:0, one launch (start us, length us, event | category | flops | bytes accessed | tf_op | source)
XLA Modules:
  0.0 227.5 jit_solution(6988182918797164582)
XLA Ops:
  7.2 0.0 copy-start
  7.2 0.0 all-gather.10.cloned.1.call-start
  7.2 1.2 fusion.1
  8.5 1.8 fusion.3
  10.3 0.0 all-gather.10.cloned.1.call-update
  10.3 1.2 dynamic-slice
  12.2 0.9 dynamic-update-slice
  13.1 13.1 %all-reduce = s32[512]{0:T(512)S(1)} all-reduce(s32[512]{0:T(512)S(1)} %dynamic-update-slice), channel_id=1, replica_groups=mesh['req'=8,'tp'=4] {'req'}, use_global_device_ids=true, to_apply=%add | all-reduce | flops 512 | bytes 4096
  26.2 36.2 %all-gather.10.cloned.1.call-done = bf16[512,2048]{1,0:T(8,128)(2,1)} async-done(((bf16[64,2048]{1,0:T(8,128)(2,1)}), bf16[512,2048]{1,0:T(8,128)(2,1)}) %all-gather.10.cloned.1.call-update) | async-done | bytes 2097168 | tf_op jit(solution)/shard_map/all_gather | solution.py:40
  62.4 0.0 copy-done
  62.4 2.6 %fusion.4 = (f32[512]{0:T(512)S(1)}, f32[512,384]{0,1:T(8,128)S(1)}) fusion(bf16[512,2048]{1,0:T(8,128)(2,1)} %all-gather.10.cloned.1.call-done, bf16[2048,384]{1,0:T(8,128)(2,1)S(1)} %copy-done), kind=kOutput, calls=%fused_computation.27 | convolution fusion | flops 805502464 | bytes 4458496 | tf_op jit(solution)/shard_map/dot_general | solution.py:39
  65.1 0.0 copy-start.1
  65.1 39.2 %all-gather.4 = f32[32,1,512]{2,1,0:T(1,128)S(1)} all-gather(f32[1,1,512]{2,1,0:T(1,128)S(1)} %bitcast.49), channel_id=2, replica_groups=mesh['req'=8,'tp'=4] {'req','tp'}, dimensions={0}, use_global_device_ids=true | all-gather | bytes 67584 | tf_op jit(solution)/shard_map/all_gather | solution.py:8
  104.3 0.3 multiply_reduce_fusion
  104.5 36.8 %all-gather.5 = f32[32,1,512]{2,1,0:T(1,128)S(1)} all-gather(f32[1,1,512]{2,1,0:T(1,128)S(1)} %bitcast.51), channel_id=3, replica_groups=mesh['req'=8,'tp'=4] {'req','tp'}, dimensions={0}, use_global_device_ids=true | all-gather | bytes 67584 | tf_op jit(solution)/shard_map/all_gather | solution.py:8
  141.3 38.1 %all-gather.6 = f32[32,1,512]{2,1,0:T(1,128)S(1)} all-gather(f32[1,1,512]{2,1,0:T(1,128)S(1)} %bitcast.50), channel_id=4, replica_groups=mesh['req'=8,'tp'=4] {'req','tp'}, dimensions={0}, use_global_device_ids=true | all-gather | bytes 67584 | tf_op jit(solution)/shard_map/all_gather | solution.py:8
  179.5 36.8 %all-gather.7 = f32[32,1,512]{2,1,0:T(1,128)S(1)} all-gather(f32[1,1,512]{2,1,0:T(1,128)S(1)} %bitcast.48), channel_id=5, replica_groups=mesh['req'=8,'tp'=4] {'req','tp'}, dimensions={0}, use_global_device_ids=true | all-gather | bytes 67584 | tf_op jit(solution)/shard_map/all_gather | solution.py:8
  216.4 3.6 %while.16 = (s32[]{:T(128)}, f32[512]{0:T(512)S(1)}, f32[512]{0:T(512)S(1)}, f32[512]{0:T(512)S(1)}, f32[512]{0:T(512)S(1)}, /*index=5*/f32[31,512]{1,0:T(8,128)...) while((s32[]{:T(128)}, f32[512]{0:T(512)S(1)}, f32[512]{0:T(512)S(1)}, ...), condition=%wide.region_6.7_spmd, body=%wide.region_5.6_spmd.sunk | while | flops 6146 | bytes 51317 | solution.py:11
  220.0 0.0 copy-done.1
  220.0 0.6 subtract_multiply_fusion
  (201 shorter events, 2.3 us)
Async XLA Ops:
  7.2 55.3 %copy-start = (bf16[2048,384]{1,0:T(8,128)(2,1)S(1)}, bf16[2048,384]{1,0:T(8,128)(2,1)}, u32[]{:S(2)}) copy-start(bf16[2048,384]{1,0:T(8,128)(2,1)} %param.9) | copy-start | bytes 4718596
  7.2 55.2 %all-gather.10.cloned.1.call-start = ((), (), s32[]{:S(2)}) async-start(), calls=%async_computation | async-start | bytes 2359296 | tf_op jit(solution)/shard_map/all_gather | solution.py:40
  65.1 154.9 %copy-start.1 = (s32[64]{0:T(128)S(1)}, s32[64]{0:T(128)}, u32[]{:S(2)}) copy-start(s32[64]{0:T(128)} %param.11) | copy-start | bytes 772
Sparse Core Ops, SparseCore 0:
  10.4 51.9 all-gather.9
where the time goes:
time: 228 us; the launch traced here: 227 us
  blocking collectives  164 us (72%)
  waiting for transfers between devices  36.3 us (16%)
  between operations  14.8 us (6%)
  other arithmetic  5.27 us (2%)
  local copies, waits for them, and re-layouts  3.05 us (1%)
  matrix products  2.63 us (1%)
    all_gather x4, blocking collectives, combined_all(): pieces = jax.tree.map(lambda part: lax.all_gather(part, axis), value)  151 us
    all_gather x1, waiting for transfers between devices, body(): lax.all_gather(normed, 'req', axis=0, tiled=True)  36.2 us
    unnamed x1, blocking collectives  13.1 us
  transfers between devices with their start and end apart: 1, of which 1 were waited for; matrix products, arithmetic and copies ran while one was open for 1% of the time, Pallas kernels for 0%

commit v1 on v0

v1 whole, which is shorter than its diff:
```python
import functools

import jax
import jax.numpy as jnp
from jax import lax
from jax.experimental import pallas as pl
from jax.experimental.pallas import tpu as pltpu
from jax.sharding import PartitionSpec as P

MESH = pl.DeviceIdType.MESH
EPS = 1e-05


def general_body(hidden, norm_gain, head_weight, targets, pad_mask):
    slots = hidden.shape[0]
    voc_local = head_weight.shape[1]
    tp_count = lax.axis_size("tp")
    voc_start = (lax.axis_index("req") * tp_count + lax.axis_index("tp")) * voc_local
    wide = hidden.astype(jnp.float32)
    scale = lax.rsqrt(jnp.mean(wide * wide, axis=1, keepdims=True) + EPS)
    normed = (wide * scale * norm_gain[None, :]).astype(jnp.bfloat16)
    columns = lax.broadcasted_iota(jnp.int32, (1, voc_local), 1)
    all_targets = lax.all_gather(targets, "req", axis=0, tiled=True)
    logits = jnp.dot(
        lax.all_gather(normed, "req", axis=0, tiled=True),
        head_weight,
        preferred_element_type=jnp.float32,
    )
    top = jnp.max(logits, axis=1)
    expo = jnp.exp(logits - top[:, None])
    local = all_targets - voc_start
    picked = jnp.sum(jnp.where(columns == local[:, None], logits, 0.0), axis=1)
    stats = jnp.stack([top, jnp.sum(expo, axis=1), jnp.sum(expo * logits, axis=1), picked])
    every = lax.all_gather(stats, ("req", "tp"))
    own = lax.axis_index("req") * slots
    every = lax.dynamic_slice_in_dim(every, own, slots, 2)
    top_all = jnp.max(every[:, 0], axis=0)
    share = jnp.exp(every[:, 0] - top_all[None])
    total = jnp.sum(every[:, 1] * share, axis=0)
    weighted = jnp.sum(every[:, 2] * share, axis=0)
    lse = top_all + jnp.log(total)
    live = pad_mask.astype(jnp.float32)
    logprob = (jnp.sum(every[:, 3], axis=0) - lse) * live
    entropy = (lse - weighted / total) * live
    return (logprob, entropy)


X, A1, A2, A3, B1, B2, B3 = range(7)
Y_OF = {A2: 7, A3: 8, B1: 9, B2: 10, B3: 11}
CORE_HALF = {X: 12, A1: 13}
CORE_NEAR = {A2: 14, A3: 15, B1: 16, B2: 17, B3: 18}
CORE_FAR = {A2: 19, A3: 20, B1: 21, B2: 22, B3: 23}
N_COPIES = 24


def kernel(
    hidden, gain, weight_hbm, targets, mask,
    logprob, entropy,
    rows, weight, tgt, outbox, inbox,
    w_sem, send, recv, tgt_send, tgt_recv, stat_send, stat_recv,
):
    slots, depth = hidden.shape
    voc = weight.shape[1]
    half, quarter = slots // 2, slots // 4
    req, tp = lax.axis_index("req"), lax.axis_index("tp")
    me = req * 4 + tp
    z, x = req // 2, req % 2
    y, c = tp // 2, tp % 2

    load = pltpu.make_async_copy(weight_hbm, weight, w_sem)
    load.start()

    barrier = pltpu.get_barrier_semaphore()
    for k in range(1, 32):
        other = (me + k) % 32
        pl.semaphore_signal(barrier, inc=1, device_id=(other // 4, other % 4), device_id_type=MESH)

    def norm_half(core):
        wide = hidden[pl.ds(pl.multiple_of(core * half, half), half), :].astype(jnp.float32)
        scale = lax.rsqrt(jnp.mean(wide * wide, axis=1, keepdims=True) + EPS)
        start = pl.multiple_of(req * slots + core * half, half)
        rows[pl.ds(start, half), :] = (wide * scale * gain[...]).astype(jnp.bfloat16)

    norm_half(c)
    tgt[req] = jnp.concatenate([targets[...], jnp.zeros((1, 128 - slots), jnp.int32)], axis=1)
    pl.semaphore_wait(barrier, 31)

    z1 = z + 1 - 2 * (z % 2)
    z2 = (z + 2) % 4
    z3 = 3 - z
    xo = 1 - x
    block = {X: z * 2 + xo, A1: z1 * 2 + x, A2: z2 * 2 + x, A3: z3 * 2 + x,
             B1: z1 * 2 + xo, B2: z2 * 2 + xo, B3: z3 * 2 + xo}
    x_dev, y_dev, core_dev = (z * 2 + xo, tp), (req, (1 - y) * 2 + c), (req, y * 2 + 1 - c)

    def half_rows(b, core):
        return rows.at[pl.ds(pl.multiple_of(b * slots + core * half, half), half), :]

    def quarter_rows(b, core, side):
        start = b * slots + core * half + side * quarter
        return rows.at[pl.ds(pl.multiple_of(start, quarter), quarter), :]

    started = []

    def push(piece, index, device):
        copy = pltpu.make_async_remote_copy(
            src_ref=piece, dst_ref=piece, send_sem=send.at[index], recv_sem=recv.at[index],
            device_id=device, device_id_type=MESH,
        )
        copy.start()
        started.append(copy)

    def arrived(piece, index):
        pltpu.make_async_copy(piece, piece, recv.at[index]).wait()

    push(quarter_rows(req, c, y), A3, (block[A3], tp))
    push(half_rows(req, c), X, x_dev)
    push(quarter_rows(req, c, y), A2, (block[A2], tp))
    push(half_rows(req, c), A1, (block[A1], tp))
    tgt_copies = []
    for k in range(1, 8):
        other = (req + k) % 8
        copy = pltpu.make_async_remote_copy(
            src_ref=tgt.at[req], dst_ref=tgt.at[req], send_sem=tgt_send.at[k - 1],
            recv_sem=tgt_recv.at[k - 1], device_id=(other, tp), device_id_type=MESH,
        )
        copy.start()
        tgt_copies.append(copy)
    norm_half(1 - c)

    eye = lax.broadcasted_iota(jnp.int32, (slots, slots), 0) == lax.broadcasted_iota(
        jnp.int32, (slots, slots), 1)
    eye2 = lax.broadcasted_iota(jnp.int32, (2 * slots, 2 * slots), 0) == lax.broadcasted_iota(
        jnp.int32, (2 * slots, 2 * slots), 1)
    voc_ids = lax.broadcasted_iota(jnp.int32, (2 * slots, voc), 1) + me * voc

    def compute(index, plane):
        lhs = rows[pl.ds(pl.multiple_of(plane * 2 * slots, 2 * slots), 2 * slots), :]
        logits = jnp.dot(lhs, weight[...], preferred_element_type=jnp.float32)
        wanted = jnp.concatenate([
            jnp.sum(jnp.where(eye, tgt[plane * 2 + i][:, :slots], 0), axis=1, keepdims=True)
            for i in range(2)
        ], axis=0)
        top = jnp.max(logits, axis=1, keepdims=True)
        expo = jnp.exp(logits - top)
        parts = (
            top,
            jnp.sum(expo, axis=1, keepdims=True),
            jnp.sum(expo * logits, axis=1, keepdims=True),
            jnp.sum(jnp.where(voc_ids == wanted, logits, 0.0), axis=1, keepdims=True),
        )
        outbox[index] = jnp.concatenate(
            [jnp.sum(jnp.where(eye2, part, 0.0), axis=0, keepdims=True) for part in parts], axis=0)
        for k in range(8):
            if index == 0:
                if k == 0:
                    inbox[me] = outbox[index]
                    continue
                other = z * 8 + (me + k) % 8
            else:
                other = plane * 8 + (me + k) % 8
            pltpu.make_async_remote_copy(
                src_ref=outbox.at[index], dst_ref=inbox.at[me], send_sem=stat_send,
                recv_sem=stat_recv, device_id=(other // 4, other % 4), device_id_type=MESH,
            ).start()

    def near(kind):
        piece = quarter_rows(block[kind], c, y)
        arrived(piece, kind)
        if kind in (A2, A3):
            push(piece, kind - A1 + B1, x_dev)
        push(piece, Y_OF[kind], y_dev)
        push(piece, CORE_NEAR[kind], core_dev)

    def far(kind):
        piece = quarter_rows(block[kind], c, 1 - y)
        arrived(piece, Y_OF[kind])
        push(piece, CORE_FAR[kind], core_dev)

    def from_core(kind):
        if kind in CORE_HALF:
            arrived(half_rows(block[kind], 1 - c), CORE_HALF[kind])
        else:
            arrived(quarter_rows(block[kind], 1 - c, y), CORE_NEAR[kind])
            arrived(quarter_rows(block[kind], 1 - c, 1 - y), CORE_FAR[kind])

    arrived(half_rows(block[A1], c), A1)
    push(quarter_rows(block[A1], c, y), B1, x_dev)
    push(half_rows(block[A1], c), CORE_HALF[A1], core_dev)
    arrived(half_rows(block[X], c), X)
    push(half_rows(block[X], c), CORE_HALF[X], core_dev)
    near(A2)
    near(A3)
    load.wait()
    for copy in tgt_copies:
        copy.wait()
    from_core(X)
    compute(0, z)
    near(B1)
    near(B2)
    near(B3)
    far(A2)
    far(A3)
    far(B1)
    from_core(A1)
    from_core(B1)
    compute(1, z1)
    far(B2)
    far(B3)
    from_core(A2)
    from_core(B2)
    compute(2, z2)
    from_core(A3)
    from_core(B3)
    compute(3, z3)

    most = inbox.at[pl.ds(0, 31)]
    pltpu.make_async_copy(most, most, stat_recv).wait()
    every = inbox[...]
    tops = every[:, 0:1, :]
    top = jnp.max(tops, axis=0)
    share = jnp.exp(tops - top[None])
    total = jnp.sum(every[:, 1:2, :] * share, axis=0)
    weighted = jnp.sum(every[:, 2:3, :] * share, axis=0)
    picked = jnp.sum(every[:, 3:4, :], axis=0)
    lse = top + jnp.log(total)
    live = mask[...].astype(jnp.float32)
    own = lambda row: jnp.where(x == 0, row[:, :slots], row[:, slots:])
    logprob[...] = own(picked - lse) * live
    entropy[...] = own(lse - weighted / total) * live

    for copy in started:
        copy.wait_send()
    pltpu.make_async_copy(most, most, stat_send).wait()


def fused_body(hidden, norm_gain, head_weight, targets, pad_mask):
    slots, depth = hidden.shape
    voc = head_weight.shape[1]
    vmem = pl.BlockSpec(memory_space=pltpu.VMEM)
    row = jax.ShapeDtypeStruct((1, slots), jnp.float32)
    logprob, entropy = pl.pallas_call(
        kernel,
        out_shape=(row, row),
        in_specs=[vmem, vmem, pl.BlockSpec(memory_space=pl.ANY), vmem, vmem],
        out_specs=(vmem, vmem),
        scratch_shapes=[
            pltpu.VMEM((8 * slots, depth), jnp.bfloat16),
            pltpu.VMEM((depth, voc), jnp.bfloat16),
            pltpu.VMEM((8, 1, 128), jnp.int32),
            pltpu.VMEM((4, 4, 128), jnp.float32),
            pltpu.VMEM((32, 4, 128), jnp.float32),
            pltpu.SemaphoreType.DMA,
            pltpu.SemaphoreType.DMA((N_COPIES,)),
            pltpu.SemaphoreType.DMA((N_COPIES,)),
            pltpu.SemaphoreType.DMA((7,)),
            pltpu.SemaphoreType.DMA((7,)),
            pltpu.SemaphoreType.DMA,
            pltpu.SemaphoreType.DMA,
        ],
        compiler_params=pltpu.CompilerParams(
            collective_id=0, has_side_effects=True, vmem_limit_bytes=32 * 1024 * 1024),
    )(hidden, norm_gain.reshape(1, depth), head_weight, targets.reshape(1, slots),
      pad_mask.reshape(1, slots))
    return (logprob.reshape(slots), entropy.reshape(slots))


def solution(mesh):
    fused = mesh.shape["req"] == 8 and mesh.shape["tp"] == 4
    return jax.shard_map(
        fused_body if fused else general_body,
        mesh=mesh,
        in_specs=(P("req", None), P(), P(None, ("req", "tp")), P("req"), P("req")),
        out_specs=(P("req"), P("req")),
        check_vma=False,
    )
```

time: 228 us -> 36.9 us (0.16)
  blocking collectives: 164 us -> 0 us
  waiting for transfers between devices: 36.3 us -> 0 us
  Pallas kernels: 0 us -> 30.6 us
  between operations: 14.8 us -> 0.65 us
  other arithmetic: 5.27 us -> 0 us
  matrix products: 2.63 us -> 0 us
  local copies, waits for them, and re-layouts: 3.05 us -> 5.38 us
    all_gather x4 -> x0, blocking collectives: 151 us -> none  [combined_all(): pieces = jax.tree.map(lambda part: lax.all_gather(part, axis), value)]
    all_gather x1 -> x0, waiting for transfers between devices: 36.2 us -> none  [body(): lax.all_gather(normed, 'req', axis=0, tiled=True)]
    pallas_call x0 -> x1, Pallas kernels: none -> 30.6 us  [fused_body(): pl.pallas_call(kernel, out_shape=(row, row), in_specs=[vmem, vmem, pl.Blo...]
    unnamed x1 -> x0, blocking collectives: 13.1 us -> none
    unnamed x11 -> x12, local copies, waits for them, and re-layouts: 2.15 us -> 5.38 us
    dot_general x1 -> x0, matrix products: 2.63 us -> none  [body(): jnp.dot(lax.all_gather(normed, 'req', axis=0, tiled=True), head_weight, p...]
  transfers between devices with their start and end apart: 1 -> 0, of which waited for: 1 -> 0; matrix products, arithmetic and copies ran while one was open for 1% -> 0% of each run, Pallas kernels for 0% -> 0%
where the time goes in v1:
time: 36.9 us; the launch traced here: 36.6 us
  Pallas kernels  30.6 us (83%)
  local copies, waits for them, and re-layouts  5.38 us (15%)
  between operations  0.65 us (2%)
    pallas_call x1, Pallas kernels, fused_body(): pl.pallas_call(kernel, out_shape=(row, row), in_specs=[vmem, vmem, pl.Blo...  30.6 us
    unnamed x12, local copies, waits for them, and re-layouts  5.38 us

profile of v1, /device:TPU:0, one launch (start us, length us, event | category | flops | bytes accessed | tf_op | source)
XLA Modules:
  0.0 36.6 jit_solution(612973090734470059)
XLA Ops:
  0.6 0.0 copy-start
  0.6 1.4 %copy-done = bf16[2048,384]{1,0:T(8,128)(2,1)S(1)} copy-done((bf16[2048,384]{1,0:T(8,128)(2,1)S(1)}, bf16[2048,384]{1,0:T(8,128)(2,1)}, u32[]{:S(2)}) %copy-start) | copy-done | bytes 1572888
  2.0 0.0 copy-start.1
  2.0 0.9 %copy-done.1 = bf16[64,2048]{1,0:T(8,128)(2,1)S(1)} copy-done((bf16[64,2048]{1,0:T(8,128)(2,1)S(1)}, bf16[64,2048]{1,0:T(8,128)(2,1)}, u32[]{:S(2)}) %copy-start.1) | copy-done | bytes 262168
  3.0 0.0 copy-start.2
  3.0 0.7 %copy-done.2 = f32[2048]{0:T(1024)S(1)} copy-done((f32[2048]{0:T(1024)S(1)}, f32[2048]{0:T(1024)}, u32[]{:S(2)}) %copy-start.2) | copy-done | bytes 8216
  3.7 0.0 copy-start.3
  3.7 0.7 %copy-done.3 = s32[64]{0:T(128)S(1)} copy-done((s32[64]{0:T(128)S(1)}, s32[64]{0:T(128)}, u32[]{:S(2)}) %copy-start.3) | copy-done | bytes 280
  4.3 0.0 copy-start.4
  4.3 0.7 %copy-done.4 = s32[64]{0:T(128)S(1)} copy-done((s32[64]{0:T(128)S(1)}, s32[64]{0:T(128)}, u32[]{:S(2)}) %copy-start.4) | copy-done | bytes 280
  5.0 30.6 %shard_map.68 = (f32[1,64]{1,0:T(1,128)S(1)}, f32[1,64]{1,0:T(1,128)S(1)}) custom-call(bf16[64,2048]{1,0:T(8,128)(2,1)S(1)} %copy-done.1, f32[1,2048]{1,0:T(1,128)S(1)} %bitcast.5, bf16[2048,384]{1,0:T(8,128)(2,1)S(1)} %copy-done, s32[1,64]{1,0:T(1,128)S(1)} %bitcast.6, s32[1,64]{1,0:T(1,128)S(1)} %bitcast.7), custom_call_target="tpu_custom_call" | custom-call | tf_op jit(solution)/shard_map/pallas_call | solution.py:242
  35.6 0.5 %copy.9 = f32[64]{0:T(128)} copy(f32[64]{0:T(128)S(1)} %bitcast.9) | data formatting | bytes 512
  36.1 0.5 %copy.10 = f32[64]{0:T(128)} copy(f32[64]{0:T(128)S(1)} %bitcast.8) | data formatting | bytes 512
Async XLA Ops:
  0.6 1.4 %copy-start = (bf16[2048,384]{1,0:T(8,128)(2,1)S(1)}, bf16[2048,384]{1,0:T(8,128)(2,1)}, u32[]{:S(2)}) copy-start(bf16[2048,384]{1,0:T(8,128)(2,1)} %weight_hbm.1) | copy-start | bytes 4718596
  2.0 0.9 %copy-start.1 = (bf16[64,2048]{1,0:T(8,128)(2,1)S(1)}, bf16[64,2048]{1,0:T(8,128)(2,1)}, u32[]{:S(2)}) copy-start(bf16[64,2048]{1,0:T(8,128)(2,1)} %hidden.1) | copy-start | bytes 786436
  3.0 0.7 %copy-start.2 = (f32[2048]{0:T(1024)S(1)}, f32[2048]{0:T(1024)}, u32[]{:S(2)}) copy-start(f32[2048]{0:T(1024)} %param.6) | copy-start | bytes 24580
  3.7 0.7 %copy-start.3 = (s32[64]{0:T(128)S(1)}, s32[64]{0:T(128)}, u32[]{:S(2)}) copy-start(s32[64]{0:T(128)} %param.8) | copy-start | bytes 772
  4.3 0.7 %copy-start.4 = (s32[64]{0:T(128)S(1)}, s32[64]{0:T(128)}, u32[]{:S(2)}) copy-start(s32[64]{0:T(128)} %param.9) | copy-start | bytes 772

commit v2 on v1

--- a/solution.py
+++ b/solution.py
@@ -45,19 +45,18 @@
     return (logprob, entropy)
 
 
-X, A1, A2, A3, B1, B2, B3 = range(7)
-Y_OF = {A2: 7, A3: 8, B1: 9, B2: 10, B3: 11}
-CORE_HALF = {X: 12, A1: 13}
-CORE_NEAR = {A2: 14, A3: 15, B1: 16, B2: 17, B3: 18}
-CORE_FAR = {A2: 19, A3: 20, B1: 21, B2: 22, B3: 23}
-N_COPIES = 24
+X, A1, A2, A3, B1, B2, B3, XP, A1P, A2P, A3P, B1P, B2P, B3P = range(14)
+OTHER_Y = {X: XP, A1: A1P, A2: A2P, A3: A3P, B1: B1P, B2: B2P, B3: B3P}
+CORE = 14
+N_COPIES = 28
+SUBS = 1
 
 
 def kernel(
-    hidden, gain, weight_hbm, targets, mask,
-    logprob, entropy,
-    rows, weight, tgt, outbox, inbox,
-    w_sem, send, recv, tgt_send, tgt_recv, stat_send, stat_recv,
+    hidden_hbm, gain_hbm, weight_hbm, targets_hbm,
+    result,
+    hidden, gain, targets, rows, weight, tgt, outbox, inbox,
+    in_sems, w_sem, send, recv, tgt_send, tgt_recv, stat_send, stat_recv,
 ):
     slots, depth = hidden.shape
     voc = weight.shape[1]
@@ -67,6 +66,13 @@
     z, x = req // 2, req % 2
     y, c = tp // 2, tp % 2
 
+    small = [
+        pltpu.make_async_copy(hidden_hbm, hidden, in_sems.at[0]),
+        pltpu.make_async_copy(gain_hbm, gain, in_sems.at[1]),
+        pltpu.make_async_copy(targets_hbm, targets, in_sems.at[2]),
+    ]
+    for copy in small:
+        copy.start()
     load = pltpu.make_async_copy(weight_hbm, weight, w_sem)
     load.start()
 
@@ -81,6 +87,8 @@
         start = pl.multiple_of(req * slots + core * half, half)
         rows[pl.ds(start, half), :] = (wide * scale * gain[...]).astype(jnp.bfloat16)
 
+    for copy in small:
+        copy.wait()
     norm_half(c)
     tgt[req] = jnp.concatenate([targets[...], jnp.zeros((1, 128 - slots), jnp.int32)], axis=1)
     pl.semaphore_wait(barrier, 31)
@@ -92,17 +100,20 @@
     block = {X: z * 2 + xo, A1: z1 * 2 + x, A2: z2 * 2 + x, A3: z3 * 2 + x,
              B1: z1 * 2 + xo, B2: z2 * 2 + xo, B3: z3 * 2 + xo}
     x_dev, y_dev, core_dev = (z * 2 + xo, tp), (req, (1 - y) * 2 + c), (req, y * 2 + 1 - c)
-
-    def half_rows(b, core):
-        return rows.at[pl.ds(pl.multiple_of(b * slots + core * half, half), half), :]
-
-    def quarter_rows(b, core, side):
-        start = b * slots + core * half + side * quarter
-        return rows.at[pl.ds(pl.multiple_of(start, quarter), quarter), :]
+    diag_dev = (z * 2 + xo, (1 - y) * 2 + c)
+
+    for kind in OTHER_Y:
+        block[OTHER_Y[kind]] = block[kind]
+
+    def piece_of(b, core, side, sub):
+        start = pl.multiple_of(b * slots + core * half + side * quarter, quarter)
+        width = depth // SUBS
+        return rows.at[pl.ds(start, quarter), pl.ds(sub * width, width)]
 
     started = []
 
-    def push(piece, index, device):
+    def push(piece, kind, sub, device):
+        index = kind * SUBS + sub
         copy = pltpu.make_async_remote_copy(
             src_ref=piece, dst_ref=piece, send_sem=send.at[index], recv_sem=recv.at[index],
             device_id=device, device_id_type=MESH,
@@ -110,13 +121,19 @@
         copy.start()
         started.append(copy)
 
-    def arrived(piece, index):
-        pltpu.make_async_copy(piece, piece, recv.at[index]).wait()
-
-    push(quarter_rows(req, c, y), A3, (block[A3], tp))
-    push(half_rows(req, c), X, x_dev)
-    push(quarter_rows(req, c, y), A2, (block[A2], tp))
-    push(half_rows(req, c), A1, (block[A1], tp))
+    def arrived(piece, kind, sub):
+        pltpu.make_async_copy(piece, piece, recv.at[kind * SUBS + sub]).wait()
+
+    z_dev = {A1: (block[A1], tp), A2: (block[A2], tp), A3: (block[A3], tp), X: x_dev}
+
+    def give(kind):
+        target, side = (kind, y) if kind < XP else (kind - XP, 1 - y)
+        for sub in range(SUBS):
+            push(piece_of(req, c, side, sub), kind, sub, z_dev[target])
+
+    give(A3)
+    give(X)
+    give(A1)
     tgt_copies = []
     for k in range(1, 8):
         other = (req + k) % 8
@@ -127,6 +144,8 @@
         copy.start()
         tgt_copies.append(copy)
     norm_half(1 - c)
+    started.pop(0).wait_send()
+    give(A2)
 
     eye = lax.broadcasted_iota(jnp.int32, (slots, slots), 0) == lax.broadcasted_iota(
         jnp.int32, (slots, slots), 1)
@@ -152,7 +171,7 @@
         outbox[index] = jnp.concatenate(
             [jnp.sum(jnp.where(eye2, part, 0.0), axis=0, keepdims=True) for part in parts], axis=0)
         for k in range(8):
-            if index == 0:
+            if plane is z:
                 if k == 0:
                     inbox[me] = outbox[index]
                     continue
@@ -164,55 +183,42 @@
                 recv_sem=stat_recv, device_id=(other // 4, other % 4), device_id_type=MESH,
             ).start()
 
-    def near(kind):
-        piece = quarter_rows(block[kind], c, y)
-        arrived(piece, kind)
-        if kind in (A2, A3):
-            push(piece, kind - A1 + B1, x_dev)
-        push(piece, Y_OF[kind], y_dev)
-        push(piece, CORE_NEAR[kind], core_dev)
-
-    def far(kind):
-        piece = quarter_rows(block[kind], c, 1 - y)
-        arrived(piece, Y_OF[kind])
-        push(piece, CORE_FAR[kind], core_dev)
-
-    def from_core(kind):
-        if kind in CORE_HALF:
-            arrived(half_rows(block[kind], 1 - c), CORE_HALF[kind])
-        else:
-            arrived(quarter_rows(block[kind], 1 - c, y), CORE_NEAR[kind])
-            arrived(quarter_rows(block[kind], 1 - c, 1 - y), CORE_FAR[kind])
-
-    arrived(half_rows(block[A1], c), A1)
-    push(quarter_rows(block[A1], c, y), B1, x_dev)
-    push(half_rows(block[A1], c), CORE_HALF[A1], core_dev)
-    arrived(half_rows(block[X], c), X)
-    push(half_rows(block[X], c), CORE_HALF[X], core_dev)
-    near(A2)
-    near(A3)
+    routes = {A1: [(B1, x_dev)], A2: [(B2, x_dev), (A2P, y_dev)], A3: [(B3, x_dev), (A3P, y_dev)], B1: [(B1P, y_dev)], B2: [(B2P, y_dev)], B3: [(B3P, y_dev)]}
+
+    def take(*kinds):
+        for kind in kinds:
+            for sub in range(SUBS):
+                piece = piece_of(block[kind], c, y if kind < XP else 1 - y, sub)
+                arrived(piece, kind, sub)
+                for later, device in routes.get(kind, ()):
+                    push(piece, later, sub, device)
+                push(piece, CORE + kind, sub, core_dev)
+
+    def from_core(*kinds):
+        for kind in kinds:
+            for side, k in ((y, kind), (1 - y, OTHER_Y[kind])):
+                for sub in range(SUBS):
+                    arrived(piece_of(block[kind], 1 - c, side, sub), CORE + k, sub)
+
+    take(A3)
+    give(A1P)
+    take(X, A2, A1)
+    give(XP)
+    take(B3, A3P, B2, A2P, B1)
     load.wait()
     for copy in tgt_copies:
         copy.wait()
+    take(B3P)
+    from_core(A3, B3)
+    compute(0, z3)
+    take(XP, A1P, B2P)
+    from_core(A2, B2)
+    compute(1, z2)
+    take(B1P)
     from_core(X)
-    compute(0, z)
-    near(B1)
-    near(B2)
-    near(B3)
-    far(A2)
-    far(A3)
-    far(B1)
-    from_core(A1)
-    from_core(B1)
-    compute(1, z1)
-    far(B2)
-    far(B3)
-    from_core(A2)
-    from_core(B2)
-    compute(2, z2)
-    from_core(A3)
-    from_core(B3)
-    compute(3, z3)
+    compute(2, z)
+    from_core(A1, B1)
+    compute(3, z1)
 
     most = inbox.at[pl.ds(0, 31)]
     pltpu.make_async_copy(most, most, stat_recv).wait()
@@ -224,10 +230,8 @@
     weighted = jnp.sum(every[:, 2:3, :] * share, axis=0)
     picked = jnp.sum(every[:, 3:4, :], axis=0)
     lse = top + jnp.log(total)
-    live = mask[...].astype(jnp.float32)
-    own = lambda row: jnp.where(x == 0, row[:, :slots], row[:, slots:])
-    logprob[...] = own(picked - lse) * live
-    entropy[...] = own(lse - weighted / total) * live
+    both = jnp.concatenate([picked - lse, lse - weighted / total], axis=0)
+    result[...] = jnp.where(x == 0, both[:, :slots], both[:, slots:])
 
     for copy in started:
         copy.wait_send()
@@ -238,31 +242,35 @@
     slots, depth = hidden.shape
     voc = head_weight.shape[1]
     vmem = pl.BlockSpec(memory_space=pltpu.VMEM)
-    row = jax.ShapeDtypeStruct((1, slots), jnp.float32)
-    logprob, entropy = pl.pallas_call(
+    hbm = pl.BlockSpec(memory_space=pltpu.HBM)
+    result = pl.pallas_call(
         kernel,
-        out_shape=(row, row),
-        in_specs=[vmem, vmem, pl.BlockSpec(memory_space=pl.ANY), vmem, vmem],
-        out_specs=(vmem, vmem),
+        out_shape=jax.ShapeDtypeStruct((2, slots), jnp.float32),
+        in_specs=[hbm] * 4,
+        out_specs=vmem,
         scratch_shapes=[
+            pltpu.VMEM((slots, depth), jnp.bfloat16),
+            pltpu.VMEM((1, depth), jnp.float32),
+            pltpu.VMEM((1, slots), jnp.int32),
             pltpu.VMEM((8 * slots, depth), jnp.bfloat16),
             pltpu.VMEM((depth, voc), jnp.bfloat16),
             pltpu.VMEM((8, 1, 128), jnp.int32),
             pltpu.VMEM((4, 4, 128), jnp.float32),
             pltpu.VMEM((32, 4, 128), jnp.float32),
+            pltpu.SemaphoreType.DMA((3,)),
             pltpu.SemaphoreType.DMA,
-            pltpu.SemaphoreType.DMA((N_COPIES,)),
-            pltpu.SemaphoreType.DMA((N_COPIES,)),
+            pltpu.SemaphoreType.DMA((N_COPIES * SUBS,)),
+            pltpu.SemaphoreType.DMA((N_COPIES * SUBS,)),
             pltpu.SemaphoreType.DMA((7,)),
             pltpu.SemaphoreType.DMA((7,)),
             pltpu.SemaphoreType.DMA,
             pltpu.SemaphoreType.DMA,
         ],
         compiler_params=pltpu.CompilerParams(
-            collective_id=0, has_side_effects=True, vmem_limit_bytes=32 * 1024 * 1024),
-    )(hidden, norm_gain.reshape(1, depth), head_weight, targets.reshape(1, slots),
-      pad_mask.reshape(1, slots))
-    return (logprob.reshape(slots), entropy.reshape(slots))
+            collective_id=0, has_side_effects=True, vmem_limit_bytes=60 * 1024 * 1024),
+    )(hidden, norm_gain.reshape(1, depth), head_weight, targets.reshape(1, slots))
+    live = pad_mask.astype(jnp.float32)
+    return (result[0] * live, result[1] * live)
 
 
 def solution(mesh):

time: 36.9 us -> 31 us (0.84)
  local copies, waits for them, and re-layouts: 5.38 us -> 0.01 us
  Pallas kernels: 30.6 us -> 28.9 us
  other arithmetic: 0 us -> 1.25 us
    unnamed x12 -> x2, local copies, waits for them, and re-layouts: 5.38 us -> 0.01 us
    pallas_call x1, Pallas kernels: 30.6 us -> 28.9 us  [fused_body(): pl.pallas_call(kernel, out_shape=jax.ShapeDtypeStruct((2, slots), jnp.flo...]
    mul x0 -> x1, other arithmetic: none -> 1.25 us  [fused_body(): return (result[0] * live, result[1] * live)]
where the time goes in v2:
time: 31 us; the launch traced here: 30.8 us
  Pallas kernels  28.9 us (93%)
  other arithmetic  1.25 us (4%)
  between operations  0.65 us (2%)
    pallas_call x1, Pallas kernels, fused_body(): pl.pallas_call(kernel, out_shape=jax.ShapeDtypeStruct((2, slots), jnp.flo...  28.9 us
    mul x1, other arithmetic, fused_body(): return (result[0] * live, result[1] * live)  1.25 us

profile of v2, /device:TPU:0, one launch (start us, length us, event | category | flops | bytes accessed | tf_op | source)
XLA Modules:
  0.0 30.8 jit_solution(7251413144496115992)
XLA Ops:
  0.6 0.0 copy-start
  0.6 28.9 %shard_map.68 = f32[2,64]{1,0:T(2,128)} custom-call(bf16[64,2048]{1,0:T(8,128)(2,1)} %hidden_hbm.1, f32[1,2048]{1,0:T(1,128)} %bitcast.6, bf16[2048,384]{1,0:T(8,128)(2,1)} %weight_hbm.1, s32[1,64]{1,0:T(1,128)} %bitcast.7), custom_call_target="tpu_custom_call" | custom-call | tf_op jit(solution)/shard_map/pallas_call | solution.py:246
  29.6 0.0 copy-done
  29.6 1.2 %bitcast_multiply_fusion = (f32[64]{0:T(128)}, f32[64]{0:T(128)}) fusion(f32[2,64]{1,0:T(2,128)} %shard_map.68, s32[64]{0:T(128)S(1)} %copy-done), kind=kLoop, calls=%fused_computation | loop fusion | flops 192 | bytes 1280 | tf_op jit(solution)/shard_map/mul | solution.py:273
Async XLA Ops:
  0.6 28.9 %copy-start = (s32[64]{0:T(128)S(1)}, s32[64]{0:T(128)}, u32[]{:S(2)}) copy-start(s32[64]{0:T(128)} %param.9) | copy-start | bytes 772

commit v3 on v2

--- a/solution.py
+++ b/solution.py
@@ -49,7 +49,7 @@
 OTHER_Y = {X: XP, A1: A1P, A2: A2P, A3: A3P, B1: B1P, B2: B2P, B3: B3P}
 CORE = 14
 N_COPIES = 28
-SUBS = 1
+SUBS = 2
 
 
 def kernel(

time: 31 us -> 30.7 us (level)
  no operation moved by 1% of the time
where the time goes in v3:
time: 30.7 us; the launch traced here: 30.6 us
  Pallas kernels  28.7 us (93%)
  other arithmetic  1.25 us (4%)
  between operations  0.65 us (2%)
    pallas_call x1, Pallas kernels, fused_body(): pl.pallas_call(kernel, out_shape=jax.ShapeDtypeStruct((2, slots), jnp.flo...  28.7 us
    mul x1, other arithmetic, fused_body(): return (result[0] * live, result[1] * live)  1.25 us

profile of v3, /device:TPU:0, one launch (start us, length us, event | category | flops | bytes accessed | tf_op | source)
XLA Modules:
  0.0 30.6 jit_solution(7360618632544134701)
XLA Ops:
  0.6 0.0 copy-start
  0.6 28.7 %shard_map.68 = f32[2,64]{1,0:T(2,128)} custom-call(bf16[64,2048]{1,0:T(8,128)(2,1)} %hidden_hbm.1, f32[1,2048]{1,0:T(1,128)} %bitcast.6, bf16[2048,384]{1,0:T(8,128)(2,1)} %weight_hbm.1, s32[1,64]{1,0:T(1,128)} %bitcast.7), custom_call_target="tpu_custom_call" | custom-call | tf_op jit(solution)/shard_map/pallas_call | solution.py:246
  29.3 0.0 copy-done
  29.3 1.2 %bitcast_multiply_fusion = (f32[64]{0:T(128)}, f32[64]{0:T(128)}) fusion(f32[2,64]{1,0:T(2,128)} %shard_map.68, s32[64]{0:T(128)S(1)} %copy-done), kind=kLoop, calls=%fused_computation | loop fusion | flops 192 | bytes 1280 | tf_op jit(solution)/shard_map/mul | solution.py:273
Async XLA Ops:
  0.6 28.7 %copy-start = (s32[64]{0:T(128)S(1)}, s32[64]{0:T(128)}, u32[]{:S(2)}) copy-start(s32[64]{0:T(128)} %param.9) | copy-start | bytes 772
